TPU v7x, 32 devices: a whole 2x2x4 slice. The times are simulated.
32 devices in a mesh: expert: 8 (over z, x), hidden: 4 (over y, core).
Axes of the slice: x: 2, y: 2, z: 4, core: 2. Of those that a mesh axis runs over, the one named last changes fastest.
Arguments:
- tokens: bfloat16 [16384, 768], P(('expert', 'hidden')), may hold values from -6 to 6
- doc_lengths: int32 [8, 3], P('expert'), may hold values from 1 to 1024, 2048 in all within a row
- expert_ids: int32 [16384, 2], P(('expert', 'hidden')), may hold values from 0 to 7, all different within a row; in each aligned block of 512 rows (0 to 511, 512 to 1023, ...) at most 160 rows name the same one
- gain_one: float32 [768], replicated, may hold values from 0.5 to 1.5
- shift_one: float32 [768], replicated, may hold values from -1.25 to 1.25
- w_query: bfloat16 [768, 768], replicated, may hold values from -0.21875 to 0.21875
- w_key: bfloat16 [768, 768], replicated, may hold values from -0.21875 to 0.21875
- w_value: bfloat16 [768, 768], replicated, may hold values from -0.21875 to 0.21875
- w_out: bfloat16 [768, 768], replicated, may hold values from -3.5 to 3.5
- gain_two: float32 [768], replicated, may hold values from 0.5 to 1.5
- shift_two: float32 [768], replicated, may hold values from -1.25 to 1.25
- w_router: bfloat16 [768, 8], replicated, may hold values from -0.21875 to 0.21875
- w_up: bfloat16 [8, 768, 3072], P('expert', None, 'hidden'), may hold values from -0.21875 to 0.21875
- w_down: bfloat16 [8, 3072, 768], P('expert', 'hidden'), may hold values from -0.109375 to 0.109375
- out_grad: bfloat16 [16384, 768], P(('expert', 'hidden')), may hold values from -6 to 6
Outputs:
- output: bfloat16 [16384, 768], P(('expert', 'hidden'))
- input_grad: bfloat16 [16384, 768], P(('expert', 'hidden'))
- gain_one_grad: float32 [768], replicated
- shift_one_grad: float32 [768], replicated
- w_query_grad: float32 [768, 768], replicated
- w_key_grad: float32 [768, 768], replicated
- w_value_grad: float32 [768, 768], replicated
- w_out_grad: float32 [768, 768], replicated
- gain_two_grad: float32 [768], replicated
- shift_two_grad: float32 [768], replicated
- w_router_grad: float32 [768, 8], replicated
- w_up_grad: float32 [8, 768, 3072], P('expert', None, 'hidden')
- w_down_grad: float32 [8, 3072, 768], P('expert', 'hidden')
- load: float32 [8], replicated
Inputs may be any that keep to these rules, and one draw needn't show every extreme that they name: `doc_lengths`: the lengths of a group's documents, in order; they sum to 2048 and the longest in every group is 1024. `expert_ids`: each token names 2 different experts; among the 512 tokens of one device no expert is named more than 160 times, and in every draw some expert is named exactly 160 times by one device.
All inputs are finite; a program needn't handle non-finite values.
Results may differ from a plain program's by a relative error of at most 0.019.
Values may be sent and summed in bfloat16 or wider, within the bound.
A program may use at most 192 MiB of HBM per device.

v0:
```python
from functools import partial
import jax
import jax.numpy as jnp
from jax import lax
from jax.sharding import PartitionSpec as P

HEADS = 12
HEAD_DIM = 64
EPSILON = 1e-05
SCALE = 0.125
MASKED = -1e30
EXACT = lax.Precision.HIGHEST


def product(left, right):
    return jnp.dot(left, right, preferred_element_type=jnp.float32)


def contract(left, right, left_axis, right_axis):
    return lax.dot_general(
        left, right, (((left_axis,), (right_axis,)), ((), ())), preferred_element_type=jnp.float32
    )


def norm_parts(values):
    row_mean = jnp.mean(values, axis=-1, keepdims=True)
    centred = values - row_mean
    inverse = lax.rsqrt(jnp.mean(centred * centred, axis=-1, keepdims=True) + EPSILON)
    return (centred * inverse, inverse)


def norm_back(grad_out, normed, inverse, gain):
    grad_normed = grad_out * gain
    first_mean = jnp.mean(grad_normed, axis=-1, keepdims=True)
    second_mean = jnp.mean(grad_normed * normed, axis=-1, keepdims=True)
    return inverse * (grad_normed - first_mean - normed * second_mean)


def gelu_back(pre_act, grad_hidden):
    unused, pull = jax.vjp(partial(jax.nn.gelu, approximate=True), pre_act)
    return pull(grad_hidden)[0]


def split_heads(array):
    return array.reshape(array.shape[0], HEADS, HEAD_DIM).transpose(1, 0, 2)


def join_heads(array):
    return array.transpose(1, 0, 2).reshape(array.shape[1], HEADS * HEAD_DIM)


def shards(
    tokens,
    doc_lengths,
    expert_ids,
    gain_one,
    shift_one,
    w_query,
    w_key,
    w_value,
    w_out,
    gain_two,
    shift_two,
    w_router,
    w_up,
    w_down,
    out_grad,
):
    row_count = tokens.shape[0]
    model_width = tokens.shape[1]
    top_count = expert_ids.shape[1]
    experts = lax.axis_size("expert") * w_up.shape[0]
    capacity = max(2, row_count * top_count * 5 // (4 * experts))
    input_float = tokens.astype(jnp.float32)
    normed_one, inverse_one = norm_parts(input_float)
    h_one = (normed_one * gain_one + shift_one).astype(jnp.bfloat16)
    queries = product(h_one, w_query).astype(jnp.bfloat16)
    key_proj = product(h_one, w_key).astype(jnp.bfloat16)
    value_proj = product(h_one, w_value).astype(jnp.bfloat16)
    all_keys, all_values = (
        lax.all_gather(key_proj, "hidden", axis=0, tiled=True),
        lax.all_gather(value_proj, "hidden", axis=0, tiled=True),
    )
    key_count = all_keys.shape[0]
    doc_ends = jnp.cumsum(doc_lengths[0])
    query_pos = lax.axis_index("hidden") * row_count + jnp.arange(row_count, dtype=jnp.int32)
    key_pos = jnp.arange(key_count, dtype=jnp.int32)
    query_doc = jnp.sum((query_pos[:, None] >= doc_ends[None, :]).astype(jnp.int32), axis=1)
    key_doc = jnp.sum((key_pos[:, None] >= doc_ends[None, :]).astype(jnp.int32), axis=1)
    allowed = (query_doc[:, None] == key_doc[None, :]) & (key_pos[None, :] <= query_pos[:, None])

    def head_forward(pieces):
        q_head, k_head, v_head = pieces
        scores = jnp.where(allowed, contract(q_head, k_head, 1, 1) * SCALE, MASKED)
        top_score = jnp.max(scores, axis=1, keepdims=True)
        expd = jnp.exp(scores - top_score)
        row_total = jnp.sum(expd, axis=1, keepdims=True)
        weights = (expd / row_total).astype(jnp.bfloat16)
        return (product(weights, v_head), (top_score + jnp.log(row_total))[:, 0])

    mixture, log_total = lax.map(
        head_forward, (split_heads(queries), split_heads(all_keys), split_heads(all_values))
    )
    attended = join_heads(mixture).astype(jnp.bfloat16)
    residual = input_float + product(attended, w_out)
    normed_two, inverse_two = norm_parts(residual)
    h_two = (normed_two * gain_two + shift_two).astype(jnp.bfloat16)
    h_two_float = h_two.astype(jnp.float32)
    router_float = w_router.astype(jnp.float32)
    logits = jnp.dot(h_two_float, router_float, precision=EXACT)
    choose_table = (
        expert_ids[:, :, None] == jnp.arange(experts, dtype=jnp.int32)[None, None, :]
    ).astype(jnp.float32)
    chosen = jnp.sum(choose_table * logits[:, None, :], axis=2)
    gate_weights = jax.nn.softmax(chosen, axis=1)
    flat_ids = expert_ids.reshape(-1)
    onehot = choose_table.reshape(-1, experts).astype(jnp.int32)
    before = jnp.cumsum(onehot, axis=0) - onehot
    slot_index = jnp.sum(before * onehot, axis=1)
    counts = jnp.sum(choose_table, axis=(0, 1))
    outgoing = (
        jnp.zeros((experts, capacity, model_width), jnp.bfloat16)
        .at[flat_ids, slot_index]
        .set(jnp.repeat(h_two, top_count, axis=0))
    )
    slot_rows = lax.all_to_all(outgoing, "expert", split_axis=0, concat_axis=0, tiled=True).reshape(
        -1, model_width
    )
    rows_all = lax.all_gather(slot_rows, "hidden", axis=0, tiled=True)
    pre_act = product(rows_all, w_up[0])
    hidden_act = jax.nn.gelu(pre_act, approximate=True).astype(jnp.bfloat16)
    partial_sum = product(hidden_act, w_down[0])
    produced = lax.psum_scatter(
        partial_sum.astype(jnp.bfloat16), "hidden", scatter_dimension=0, tiled=True
    )
    returned = lax.all_to_all(
        produced.reshape(-1, capacity, model_width),
        "expert",
        split_axis=0,
        concat_axis=0,
        tiled=True,
    )
    returned_rows = (
        returned[flat_ids, slot_index]
        .reshape(row_count, top_count, model_width)
        .astype(jnp.float32)
    )
    expert_mix = jnp.sum(gate_weights[:, :, None] * returned_rows, axis=1)
    output = (residual + expert_mix).astype(jnp.bfloat16)
    grad_output = out_grad.astype(jnp.float32)
    grad_returned = (gate_weights[:, :, None] * grad_output[:, None, :]).astype(jnp.bfloat16)
    grad_gates = jnp.sum(returned_rows * grad_output[:, None, :], axis=2)
    grad_chosen = gate_weights * (
        grad_gates - jnp.sum(gate_weights * grad_gates, axis=1, keepdims=True)
    )
    grad_logits = jnp.sum(grad_chosen[:, :, None] * choose_table, axis=1)
    router_grad = jnp.dot(h_two_float.T, grad_logits, precision=EXACT)
    grad_h_two = jnp.dot(grad_logits, router_float.T, precision=EXACT)
    grad_outgoing = (
        jnp.zeros((experts, capacity, model_width), jnp.bfloat16)
        .at[flat_ids, slot_index]
        .set(grad_returned.reshape(-1, model_width))
    )
    grad_slots = lax.all_to_all(
        grad_outgoing, "expert", split_axis=0, concat_axis=0, tiled=True
    ).reshape(-1, model_width)
    trainable = (lax.axis_index("expert") >= experts // 2).astype(jnp.float32)
    grad_all = lax.all_gather(grad_slots, "hidden", axis=0, tiled=True)
    grad_hidden = contract(grad_all, w_down[0], 1, 1)
    down_grad = contract(hidden_act, grad_all, 0, 0)
    grad_pre = gelu_back(pre_act, grad_hidden).astype(jnp.bfloat16)
    up_grad = contract(rows_all, grad_pre, 0, 0)
    partial_in = contract(grad_pre, w_up[0], 1, 1)
    grad_in = lax.psum_scatter(
        partial_in.astype(jnp.bfloat16), "hidden", scatter_dimension=0, tiled=True
    )
    up_grad = up_grad[None] * trainable
    down_grad = down_grad[None] * trainable
    grad_back = lax.all_to_all(
        grad_in.reshape(-1, capacity, model_width),
        "expert",
        split_axis=0,
        concat_axis=0,
        tiled=True,
    )
    grad_h_two = grad_h_two + jnp.sum(
        grad_back[flat_ids, slot_index]
        .reshape(row_count, top_count, model_width)
        .astype(jnp.float32),
        axis=1,
    )
    gain_two_grad = jnp.sum(grad_h_two * normed_two, axis=0)
    shift_two_grad = jnp.sum(grad_h_two, axis=0)
    grad_residual = grad_output + norm_back(grad_h_two, normed_two, inverse_two, gain_two)
    grad_branch = grad_residual.astype(jnp.bfloat16)
    out_proj_grad = contract(attended, grad_branch, 0, 0)
    grad_attended = contract(grad_branch, w_out, 1, 1).astype(jnp.bfloat16)
    back_keys, back_values = (all_keys, all_values)

    def head_backward(pieces):
        q_head, k_head, v_head, g_head, head_total = pieces
        scores = jnp.where(allowed, contract(q_head, k_head, 1, 1) * SCALE, MASKED)
        weights = jnp.exp(scores - head_total[:, None])
        grad_weights = contract(g_head, v_head, 1, 1)
        grad_scores = (
            weights * (grad_weights - jnp.sum(weights * grad_weights, axis=1, keepdims=True))
        ).astype(jnp.bfloat16)
        grad_query = product(grad_scores, k_head) * SCALE
        grad_key = contract(grad_scores, q_head, 0, 0) * SCALE
        grad_value = contract(weights.astype(jnp.bfloat16), g_head, 0, 0)
        return (grad_query, grad_key, grad_value)

    grad_query, grad_key, grad_value = lax.map(
        head_backward,
        (
            split_heads(queries),
            split_heads(back_keys),
            split_heads(back_values),
            split_heads(grad_attended),
            log_total,
        ),
    )
    grad_key, grad_value = (
        lax.psum_scatter(
            join_heads(grad_key).astype(jnp.bfloat16), "hidden", scatter_dimension=0, tiled=True
        ).astype(jnp.float32),
        lax.psum_scatter(
            join_heads(grad_value).astype(jnp.bfloat16), "hidden", scatter_dimension=0, tiled=True
        ).astype(jnp.float32),
    )
    grad_query = join_heads(grad_query).astype(jnp.bfloat16)
    grad_key = grad_key.astype(jnp.bfloat16)
    grad_value = grad_value.astype(jnp.bfloat16)
    query_grad = contract(h_one, grad_query, 0, 0)
    key_grad = contract(h_one, grad_key, 0, 0)
    value_grad = contract(h_one, grad_value, 0, 0)
    grad_h_one = (
        contract(grad_query, w_query, 1, 1)
        + contract(grad_key, w_key, 1, 1)
        + contract(grad_value, w_value, 1, 1)
    )
    gain_one_grad = jnp.sum(grad_h_one * normed_one, axis=0)
    shift_one_grad = jnp.sum(grad_h_one, axis=0)
    input_grad = (grad_residual + norm_back(grad_h_one, normed_one, inverse_one, gain_one)).astype(
        jnp.bfloat16
    )
    totals = lax.psum(
        (
            gain_one_grad,
            shift_one_grad,
            query_grad,
            key_grad,
            value_grad,
            out_proj_grad,
            gain_two_grad,
            shift_two_grad,
            router_grad,
            counts,
        ),
        ("expert", "hidden"),
    )
    total_tokens = row_count * lax.axis_size("expert") * lax.axis_size("hidden")
    load = totals[9] * experts / (total_tokens * top_count)
    return (
        output,
        input_grad,
        totals[0],
        totals[1],
        totals[2],
        totals[3],
        totals[4],
        totals[5],
        totals[6],
        totals[7],
        totals[8],
        up_grad,
        down_grad,
        load,
    )


def solution(mesh):
    in_specs = (
        P(("expert", "hidden"), None),
        P("expert", None),
        P(("expert", "hidden"), None),
        P(),
        P(),
        P(),
        P(),
        P(),
        P(),
        P(),
        P(),
        P(),
        P("expert", None, "hidden"),
        P("expert", "hidden", None),
        P(("expert", "hidden"), None),
    )
    out_specs = (
        P(("expert", "hidden"), None),
        P(("expert", "hidden"), None),
        P(),
        P(),
        P(),
        P(),
        P(),
        P(),
        P(),
        P(),
        P(),
        P("expert", None, "hidden"),
        P("expert", "hidden", None),
        P(),
    )
    return jax.shard_map(shards, mesh=mesh, in_specs=in_specs, out_specs=out_specs, check_vma=False)
```

profile of v0, /device:TPU:0, one launch (start us, length us, event | category | flops | bytes accessed | tf_op | source)
XLA Modules:
  0.0 1053.0 jit_solution(8360045255467511472)
XLA Ops:
  10.2 3.5 convolution_convert_fusion.4
  32.1 13.0 %all-gather.5.cloned.1.call-done = bf16[2048,768]{1,0:T(8,128)(2,1)} async-done(((bf16[512,768]{1,0:T(8,128)(2,1)}), bf16[2048,768]{1,0:T(8,128)(2,1)}) %all-gather.5.cloned.1.call-update) | async-done | bytes 3145744 | tf_op jit(solution)/shard_map/all_gather | solution.py:81
  45.1 4.8 copy.68
  49.9 6.7 copy.71
  56.6 19.4 %all-gather.7.cloned.1.call-done = bf16[2048,768]{1,0:T(8,128)(2,1)} async-done(((bf16[512,768]{1,0:T(8,128)(2,1)}), bf16[2048,768]{1,0:T(8,128)(2,1)}) %all-gather.7.cloned.1.call-update) | async-done | bytes 3145744 | tf_op jit(solution)/shard_map/all_gather | solution.py:82
  76.0 4.7 copy.69
  80.7 6.5 copy.72
  88.2 85.5 %while.28 = (s32[]{:T(128)}, bf16[12,512,64]{1,2,0:T(8,128)(2,1)}, f32[12,512]{1,0:T(8,128)}, bf16[12,512,64]{2,1,0:T(8,128)(2,1)S(1)}, bf16[12,2048,64]{2,1,0:T...) while((s32[]{:T(128)}, bf16[12,512,64]{1,2,0:T(8,128)(2,1)}, ...), condition=%wide.region_8.9_spmd.clone, body=%wide.region_5.8_spmd.clone.sunk | while | flops 279969280 | bytes 13928569 | solution.py:101
  173.6 3.0 fusion.95
  181.0 7.7 scatter_custom_fusion
  188.8 51.8 %all_to_all.20 = bf16[8,160,768]{2,1,0:T(8,128)(2,1)} all-to-all(bf16[8,160,768]{2,1,0:T(8,128)(2,1)} %bitcast.191), channel_id=1, replica_groups=mesh['expert'=8,'hidden'=4] {'expert'}, dimensions={0} | all-to-all | bytes 3932160 | tf_op jit(solution)/shard_map/all_to_all | solution.py:126
  244.2 5.5 mul.265
  250.5 7.0 scatter_custom_fusion.1
  257.5 48.8 %all_to_all.21 = bf16[8,160,768]{2,1,0:T(8,128)(2,1)} all-to-all(bf16[8,160,768]{2,1,0:T(8,128)(2,1)S(1)} %bitcast.190), channel_id=1, replica_groups=mesh['expert'=8,'hidden'=4] {'expert'}, dimensions={0} | all-to-all | bytes 3932160 | tf_op jit(solution)/shard_map/all_to_all | solution.py:164
  306.6 12.8 %fusion.72 = f32[5120,768]{1,0:T(8,128)} fusion(bf16[5120,768]{1,0:T(8,128)(2,1)} %all-gather.9.cloned.1.call-done, bf16[1,768,768]{2,1,0:T(8,128)(2,1)S(1)} %copy-done), kind=kOutput, calls=%fused_computation.115 | convolution fusion | flops 6039797760 | bytes 24772608 | tf_op jit(solution)/shard_map/dot_general | solution.py:16
  319.4 40.1 %all-gather.11.cloned.1.call-done = bf16[5120,768]{1,0:T(8,128)(2,1)} async-done(((bf16[1280,768]{1,0:T(8,128)(2,1)}), bf16[5120,768]{1,0:T(8,128)(2,1)}) %all-gather.11.cloned.1.call-update) | async-done | bytes 7864336 | tf_op jit(solution)/shard_map/all_gather | solution.py:168
  359.5 19.0 %fusion.50 = bf16[5120,768]{1,0:T(8,128)(2,1)S(1)} fusion(f32[5120,768]{1,0:T(8,128)} %fusion.72, bf16[5120,768]{1,0:T(8,128)(2,1)} %all-gather.11.cloned.1.call-done, bf16[1,768,768]{2,1,0:T(8,128)(2,1)S(1)} %copy-done.40), kind=kOutput, calls=%fused_computation.67 | convolution fusion | flops 6118440960 | bytes 32636928 | tf_op jit(solution)/shard_map/dot_general | solution.py:20
  378.5 3.1 copy-done.48
  381.7 8.7 convolution_convert_fusion
  390.5 14.8 %convolution_convert_fusion.1 = bf16[5120,768]{1,0:T(8,128)(2,1)} fusion(bf16[1,768,768]{2,1,0:T(8,128)(2,1)S(1)} %copy-done.40, f32[5120,768]{1,0:T(8,128)} %fusion.72), kind=kOutput, calls=%fused_computation.70 | convolution fusion | flops 6079119360 | bytes 24772608 | tf_op jit(solution)/shard_map/dot_general | solution.py:16
  405.3 54.2 %reduce-scatter.7.cloned.1.call-done = bf16[1280,768]{1,0:T(8,128)(2,1)} async-done(((bf16[5120,768]{1,0:T(8,128)(2,1)}), bf16[1280,768]{1,0:T(8,128)(2,1)}) %reduce-scatter.7.cloned.1.call-update) | async-done | bytes 1966096 | tf_op jit(solution)/shard_map/reduce_scatter | solution.py:174
  459.5 5.5 all-to-all-start.3
  465.0 66.1 %reduce-scatter.5.cloned.1.call-done = bf16[1280,768]{1,0:T(8,128)(2,1)} async-done(((bf16[5120,768]{1,0:T(8,128)(2,1)}), bf16[1280,768]{1,0:T(8,128)(2,1)}) %reduce-scatter.5.cloned.1.call-update) | async-done | bytes 1966096 | tf_op jit(solution)/shard_map/reduce_scatter | solution.py:133
  531.1 5.6 all-to-all-start.1
  538.1 14.3 %gather_fusion.1 = bf16[1024,768]{1,0:T(8,128)(2,1)} fusion(bf16[8,160,768]{2,1,0:T(8,128)(2,1)S(1)} %all-to-all-done.3, s32[1024]{0:T(1024)S(1)} %bitcast.184), kind=kCustom, calls=%fused_computation.1 | custom fusion | bytes 3153920 | tf_op jit(solution)/shard_map/gather | solution.py:187
  552.4 4.9 reshape.365
  557.3 25.0 %all-to-all-done.1 = bf16[8,160,768]{2,1,0:T(8,128)(2,1)} async-done(((bf16[8,160,768]{2,1,0:T(8,128)(2,1)}), bf16[8,160,768]{2,1,0:T(8,128)(2,1)}, u32[]{:S(2)}, u32[]{:S(2)}) %all-to-all-start.1) | async-done | bytes 1966112 | tf_op jit(solution)/shard_map/all_to_all | solution.py:136
  582.3 19.8 %gather_fusion = bf16[1024,768]{1,0:T(8,128)(2,1)} fusion(bf16[8,160,768]{2,1,0:T(8,128)(2,1)} %all-to-all-done.1, s32[1024]{0:T(1024)S(1)} %bitcast.185), kind=kCustom, calls=%fused_computation | custom fusion | bytes 3153920 | tf_op jit(solution)/shard_map/gather | solution.py:144
  602.1 3.5 reshape.364
  605.6 9.5 multiply_reduce_fusion.1
  616.4 5.7 reduce_sum.241
  626.7 132.8 %while.29 = (s32[]{:T(128)}, bf16[12,512,64]{1,2,0:T(8,128)(2,1)S(1)}, bf16[12,2048,64]{1,2,0:T(8,128)(2,1)}, bf16[12,2048,64]{1,2,0:T(8,128)(2,1)}, bf16[12,512...) while((s32[]{:T(128)}, ...), condition=%wide.region_30.31_spmd.clone, body=%wide.region_28.30_spmd.clone.sunk | while | flops 683834880 | bytes 34630792 | solution.py:213
  651.4 3.0 multiply_reduce_fusion.11
  662.4 3.0 multiply_reduce_fusion.11
  673.5 3.0 multiply_reduce_fusion.11
  684.6 3.0 multiply_reduce_fusion.11
  706.7 3.0 multiply_reduce_fusion.11
  751.0 3.0 multiply_reduce_fusion.11
  761.0 3.7 fusion.89
  766.8 28.9 %reduce-scatter.9.cloned.1.call-done = bf16[512,768]{0,1:T(8,128)(2,1)} async-done(((bf16[2048,768]{0,1:T(8,128)(2,1)}), bf16[512,768]{0,1:T(8,128)(2,1)}) %reduce-scatter.9.cloned.1.call-update) | async-done | bytes 786448 | tf_op jit(solution)/shard_map/reduce_scatter | solution.py:224
  795.7 3.6 fusion.87
  799.3 37.1 %reduce-scatter.11.cloned.1.call-done = bf16[512,768]{0,1:T(8,128)(2,1)} async-done(((bf16[2048,768]{0,1:T(8,128)(2,1)}), bf16[512,768]{0,1:T(8,128)(2,1)}) %reduce-scatter.11.cloned.1.call-update) | async-done | bytes 786448 | tf_op jit(solution)/shard_map/reduce_scatter | solution.py:227
  836.4 3.6 fusion.85
  840.0 12.2 %multiply_bitcast_fusion.1 = f32[1,768,768]{2,1,0:T(8,128)} fusion(bf16[5120,768]{1,0:T(8,128)(2,1)} %all-gather.9.cloned.1.call-done, bf16[5120,768]{1,0:T(8,128)(2,1)} %copy-done.48, f32[]{:T(128)S(6)} %convert_element_type.180), kind=kOutput, calls=%fused_computation.78 | convolution fusion | flops 6040387584 | bytes 18087940 | tf_op jit(solution)/shard_map/dot_general | solution.py:20
  852.2 14.4 %multiply_bitcast_fusion = f32[1,768,768]{2,1,0:T(8,128)} fusion(bf16[5120,768]{1,0:T(8,128)(2,1)} %all-gather.11.cloned.1.call-done, f32[]{:T(128)S(6)} %convert_element_type.180, f32[5120,768]{1,0:T(8,128)} %fusion.72), kind=kOutput, calls=%fused_computation.77 | convolution fusion | flops 6075777024 | bytes 25952260 | tf_op jit(solution)/shard_map/dot_general | solution.py:20
  872.6 41.3 %all-reduce = (f32[768]{0:T(1024)}, f32[768]{0:T(1024)}, f32[768]{0:T(1024)}, f32[768]{0:T(1024)}, f32[768,8]{0,1:T(8,128)}, /*index=5*/f32[8]{0:T(128)S(1)}) all-reduce(f32[768]{0:T(1024)S(1)} %get-tuple-element.230, f32[768]{0:T(1024)S(1)} %get-tuple-element.235, ...), channel_id=1, replica_groups=mesh['expert'=8,'hidden'=4] {'expert','hidden'}, use_global_device_ids=true, to_apply=%region_36.37 | all-reduce | flops 9224 | bytes 73792 | tf_op jit(solution)/shard_map/psum | solution.py:247
  917.3 119.2 %all-reduce.4.cloned.1.call-done = (f32[768,768]{1,0:T(8,128)}, f32[768,768]{1,0:T(8,128)}, f32[768,768]{1,0:T(8,128)}, f32[768,768]{1,0:T(8,128)}) async-done(((f32[768,768]{1,0:T(8,128)}, f32[768,768]{1,0:T(8,128)}, f32[768,768]{1,0:T(8,128)}, f32[768,768]{1,0:T(8,128)}), (f32[768,768]{1,0:T(8,128)}, f32[768,768]{1,0:T(8,128)}, f32[768,768]{1,0:T(8,128)}, ...) | async-done | bytes 9437200 | tf_op jit(solution)/shard_map/psum | solution.py:247
  1036.5 3.4 copy.121
  (322 shorter events, 258.0 us)
Async XLA Ops:
  7.2 299.4 %copy-start = (bf16[1,768,768]{2,1,0:T(8,128)(2,1)S(1)}, bf16[1,768,768]{2,1,0:T(8,128)(2,1)}, u32[]{:S(2)}) copy-start(bf16[1,768,768]{2,1,0:T(8,128)(2,1)} %param.31) | copy-start | bytes 3538948
  7.2 37.9 %all-gather.5.cloned.1.call-start = ((), (), s32[]{:S(2)}) async-start(), calls=%async_computation.8 | async-start | bytes 3932160 | tf_op jit(solution)/shard_map/all_gather | solution.py:81
  8.6 12.4 %copy-start.26 = (f32[512]{0:T(512)}, f32[512]{0:T(512)S(1)}, u32[]{:S(2)}) copy-start(f32[512]{0:T(512)S(1)} %broadcast_multiply_fusion.5) | copy-start | bytes 6148
  10.2 10.9 %copy-start.30 = (f32[512]{0:T(512)}, f32[512]{0:T(512)S(1)}, u32[]{:S(2)}) copy-start(f32[512]{0:T(512)S(1)} %add_rsqrt_fusion.1) | copy-start | bytes 6148
  10.2 3.6 copy-start.4
  10.2 3.6 copy-start.17
  10.2 3.6 copy-start.32
  10.2 3.6 copy-start.45
  13.7 2.3 copy-start.25
  13.7 3.6 copy-start.47
  13.7 62.2 %all-gather.7.cloned.1.call-start = ((), (), s32[]{:S(2)}) async-start(), calls=%async_computation.9 | async-start | bytes 3932160 | tf_op jit(solution)/shard_map/all_gather | solution.py:82
  15.7 290.9 %all-gather.9.cloned.1.call-start = ((), (), s32[]{:S(2)}) async-start(), calls=%async_computation.10 | async-start | bytes 9830400 | tf_op jit(solution)/shard_map/all_gather | solution.py:129
  23.2 3.2 copy-start.39
  26.4 5.1 copy-start.34
  80.7 7.5 copy-start.35
  173.6 3.0 copy-start.12
  173.6 4.7 copy-start.24
  173.6 4.7 copy-start.38
  178.7 71.0 %copy-start.6 = (bf16[512,768]{1,0:T(8,128)(2,1)}, bf16[512,768]{1,0:T(8,128)(2,1)S(1)}, u32[]{:S(2)}) copy-start(bf16[512,768]{1,0:T(8,128)(2,1)S(1)} %add_convert_fusion.1) | copy-start | bytes 2359300
  240.6 118.9 %all-gather.11.cloned.1.call-start = ((), (), s32[]{:S(2)}) async-start(), calls=%async_computation.12 | async-start | bytes 9830400 | tf_op jit(solution)/shard_map/all_gather | solution.py:168
  244.2 5.5 copy-start.23
  306.3 53.2 %copy-start.40 = (bf16[1,768,768]{2,1,0:T(8,128)(2,1)S(1)}, bf16[1,768,768]{2,1,0:T(8,128)(2,1)}, u32[]{:S(2)}) copy-start(bf16[1,768,768]{2,1,0:T(8,128)(2,1)} %param.32) | copy-start | bytes 3538948
  306.3 153.2 %reduce-scatter.7.cloned.1.call-start = ((), (), s32[]{:S(2)}) async-start(), calls=%async_computation.13 | async-start | bytes 9830400 | tf_op jit(solution)/shard_map/reduce_scatter | solution.py:174
  378.5 3.2 copy-start.48
  390.4 140.7 %reduce-scatter.5.cloned.1.call-start = ((), (), s32[]{:S(2)}) async-start(), calls=%async_computation.11 | async-start | bytes 9830400 | tf_op jit(solution)/shard_map/reduce_scatter | solution.py:133
  459.5 71.6 %all-to-all-start.3 = ((bf16[8,160,768]{2,1,0:T(8,128)(2,1)}), bf16[8,160,768]{2,1,0:T(8,128)(2,1)S(1)}, u32[]{:S(2)}, u32[]{:S(2)}) async-start(bf16[8,160,768]{2,1,0:T(8,128)(2,1)} %bitcast.199), calls=%async_computation.5 | async-start | bytes 3932160 | tf_op jit(solution)/shard_map/all_to_all | solution.py:179
  531.1 5.7 copy-start.9
  531.1 51.2 %all-to-all-start.1 = ((bf16[8,160,768]{2,1,0:T(8,128)(2,1)}), bf16[8,160,768]{2,1,0:T(8,128)(2,1)}, u32[]{:S(2)}, u32[]{:S(2)}) async-start(bf16[8,160,768]{2,1,0:T(8,128)(2,1)} %bitcast.198), calls=%async_computation.2 | async-start | bytes 3932160 | tf_op jit(solution)/shard_map/all_to_all | solution.py:136
  536.8 258.9 %reduce-scatter.9.cloned.1.call-start = ((), (), s32[]{:S(2)}) async-start(), calls=%async_computation.14 | async-start | bytes 3932160 | tf_op jit(solution)/shard_map/reduce_scatter | solution.py:224
  616.3 5.7 copy-start.3
  616.3 5.8 copy-start.29
  622.1 1.4 copy-start.10
  622.1 1.6 copy-start.11
  623.8 1.4 copy-start.41
  759.5 1.4 copy-start.5
  759.5 1.4 copy-start.27
  759.6 76.8 %reduce-scatter.11.cloned.1.call-start = ((), (), s32[]{:S(2)}) async-start(), calls=%async_computation.15 | async-start | bytes 3932160 | tf_op jit(solution)/shard_map/reduce_scatter | solution.py:227
  760.4 276.1 %all-reduce.4.cloned.1.call-start = ((), (), s32[]{:S(2)}) async-start(), calls=%async_computation.16 | async-start | bytes 18874368 | tf_op jit(solution)/shard_map/psum | solution.py:247
  760.9 3.7 copy-start.13
  852.2 14.4 %copy-start.7 = (bf16[512,768]{1,0:T(8,128)(2,1)S(1)}, bf16[512,768]{1,0:T(8,128)(2,1)}, u32[]{:S(2)}) copy-start(bf16[512,768]{1,0:T(8,128)(2,1)} %copy-done.6) | copy-start | bytes 2359300
  852.2 14.8 %copy-start.21 = (bf16[12,512,64]{1,2,0:T(8,128)(2,1)S(1)}, bf16[12,512,64]{1,2,0:T(8,128)(2,1)}, u32[]{:S(2)}) copy-start(bf16[12,512,64]{1,2,0:T(8,128)(2,1)} %copy-done.20) | copy-start | bytes 2359300
  852.2 14.8 %copy-start.42 = (bf16[768,768]{1,0:T(8,128)(2,1)S(1)}, bf16[768,768]{1,0:T(8,128)(2,1)}, u32[]{:S(2)}) copy-start(bf16[768,768]{1,0:T(8,128)(2,1)} %param.24) | copy-start | bytes 3538948
  867.0 1.5 copy-start.44
  868.5 1.5 copy-start.19
  1036.5 3.4 copy-start.16
  1039.8 2.5 copy-start.15
  1042.4 2.5 copy-start.14
  1042.4 3.9 copy-start.1
  (12 other events, 12.6 us)
Sparse Core Ops, SparseCore 0:
  13.8 31.2 all-gather.4
  47.2 28.6 all-gather.6
  240.7 53.0 all-gather.8
  306.4 53.0 all-gather.10
  390.5 68.9 reduce-scatter.6
  462.1 68.9 reduce-scatter.4
  759.6 36.0 reduce-scatter.8
  798.4 37.9 reduce-scatter.10
  843.2 193.2 all-reduce.3
where the time goes:
time: 1060 us; the launch traced here: 1050 us
  waiting for transfers between devices  404 us (38%)
  matrix products  292 us (28%)
  blocking collectives  142 us (13%)
  local copies, waits for them, and re-layouts  134 us (13%)
  other arithmetic  54.7 us (5%)
  between operations  14.7 us (1%)
  starting transfers between devices  11.9 us (1%)
    dot_general x72, matrix products, contract(): lax.dot_general(left, right, (((left_axis,), (right_axis,)), ((), ())), p...  197 us
    psum x1, waiting for transfers between devices, shards(): lax.psum((gain_one_grad, shift_one_grad, query_grad, key_grad, value_grad...  119 us
    dot_general x30, matrix products, product(): return jnp.dot(left, right, preferred_element_type=jnp.float32)  92.8 us
    reduce_scatter x1, waiting for transfers between devices, shards(): lax.psum_scatter(partial_sum.astype(jnp.bfloat16), 'hidden', scatter_dime...  66.1 us
    reduce_scatter x1, waiting for transfers between devices, shards(): lax.psum_scatter(partial_in.astype(jnp.bfloat16), 'hidden', scatter_dimen...  54.2 us
    all_to_all x1, blocking collectives, shards(): lax.all_to_all(outgoing, 'expert', split_axis=0, concat_axis=0, tiled=True)  51.8 us
    all_to_all x1, blocking collectives, shards(): lax.all_to_all(grad_outgoing, 'expert', split_axis=0, concat_axis=0, tile...  48.8 us
    unnamed x107, local copies, waits for them, and re-layouts  41.6 us
  transfers between devices with their start and end apart: 11, of which 9 were waited for; matrix products, arithmetic and copies ran while one was open for 13% of the time, Pallas kernels for 0%

commit v1 on v0

--- a/solution.py
+++ b/solution.py
@@ -165,7 +165,23 @@
         grad_outgoing, "expert", split_axis=0, concat_axis=0, tiled=True
     ).reshape(-1, model_width)
     trainable = (lax.axis_index("expert") >= experts // 2).astype(jnp.float32)
-    grad_all = lax.all_gather(grad_slots, "hidden", axis=0, tiled=True)
+    ways, here, step = (lax.axis_size("hidden"), lax.axis_index("hidden"), grad_slots.shape[0])
+    lengths = [n * ways if d == 0 else n for d, n in enumerate(grad_slots.shape)]
+    full = lax.dynamic_update_slice_in_dim(
+        jnp.zeros(lengths, grad_slots.dtype), grad_slots, here * step, axis=0
+    )
+    going_up = going_down = grad_slots
+    for far in range(1, ways // 2 + 1):
+        going_up = lax.ppermute(going_up, "hidden", [(d, (d + 1) % ways) for d in range(ways)])
+        full = lax.dynamic_update_slice_in_dim(full, going_up, (here - far) % ways * step, axis=0)
+        if 2 * far < ways:
+            going_down = lax.ppermute(
+                going_down, "hidden", [(d, (d - 1) % ways) for d in range(ways)]
+            )
+            full = lax.dynamic_update_slice_in_dim(
+                full, going_down, (here + far) % ways * step, axis=0
+            )
+    grad_all = full
     grad_hidden = contract(grad_all, w_down[0], 1, 1)
     down_grad = contract(hidden_act, grad_all, 0, 0)
     grad_pre = gelu_back(pre_act, grad_hidden).astype(jnp.bfloat16)

time: 1060 us -> 1090 us (1.028)
  local copies, waits for them, and re-layouts: 134 us -> 147 us
  waiting for transfers between devices: 404 us -> 415 us
    ppermute x0 -> x3, waiting for transfers between devices: none -> 54.6 us  [the longest x2 54.6 us: shards(): lax.ppermute(going_up, 'hidden', [(d, (d + 1) % ways) for d in range(ways)])]
    all_gather x1 -> x0, waiting for transfers between devices: 40.1 us -> none  [shards(): grad_all = lax.all_gather(grad_slots, 'hidden', axis=0, tiled=True)]
    dynamic_update_slice x0 -> x4, local copies, waits for them, and re-layouts: none -> 11.9 us  [the longest x2 5.93 us: shards(): lax.dynamic_update_slice_in_dim(full, going_up, (here - far) % ways * ste...]
    unnamed x107 -> x123, local copies, waits for them, and re-layouts: 41.6 us -> 41.4 us
  transfers between devices with their start and end apart: 11 -> 13, of which waited for: 9 -> 10; matrix products, arithmetic and copies ran while one was open for 13% -> 13% of each run, Pallas kernels for 0% -> 0%
where the time goes in v1:
time: 1090 us; the launch traced here: 1080 us
  waiting for transfers between devices  415 us (38%)
  matrix products  293 us (27%)
  local copies, waits for them, and re-layouts  147 us (13%)
  blocking collectives  142 us (13%)
  other arithmetic  57.3 us (5%)
  between operations  15 us (1%)
  starting transfers between devices  13.4 us (1%)
    dot_general x72, matrix products, contract(): lax.dot_general(left, right, (((left_axis,), (right_axis,)), ((), ())), p...  196 us
    psum x1, waiting for transfers between devices, shards(): lax.psum((gain_one_grad, shift_one_grad, query_grad, key_grad, value_grad...  119 us
    dot_general x30, matrix products, product(): return jnp.dot(left, right, preferred_element_type=jnp.float32)  93.4 us
    reduce_scatter x1, waiting for transfers between devices, shards(): lax.psum_scatter(partial_sum.astype(jnp.bfloat16), 'hidden', scatter_dime...  66.1 us
    ppermute x2, waiting for transfers between devices, shards(): lax.ppermute(going_up, 'hidden', [(d, (d + 1) % ways) for d in range(ways)])  54.6 us
    all_to_all x1, blocking collectives, shards(): lax.all_to_all(outgoing, 'expert', split_axis=0, concat_axis=0, tiled=True)  51.8 us
    reduce_scatter x1, waiting for transfers between devices, shards(): lax.psum_scatter(partial_in.astype(jnp.bfloat16), 'hidden', scatter_dimen...  49.5 us
    all_to_all x1, blocking collectives, shards(): lax.all_to_all(grad_outgoing, 'expert', split_axis=0, concat_axis=0, tile...  49.3 us
  transfers between devices with their start and end apart: 13, of which 10 were waited for; matrix products, arithmetic and copies ran while one was open for 13% of the time, Pallas kernels for 0%

profile of v1, /device:TPU:0, one launch (start us, length us, event | category | flops | bytes accessed | tf_op | source)
XLA Modules:
  0.0 1082.8 jit_solution(18068115985048139838)
XLA Ops:
  10.2 3.5 convolution_convert_fusion.4
  31.3 13.8 %all-gather.4.cloned.1.call-done = bf16[2048,768]{1,0:T(8,128)(2,1)} async-done(((bf16[512,768]{1,0:T(8,128)(2,1)}), bf16[2048,768]{1,0:T(8,128)(2,1)}) %all-gather.4.cloned.1.call-update) | async-done | bytes 3145744 | tf_op jit(solution)/shard_map/all_gather | solution.py:81
  45.1 4.8 copy.68
  49.9 6.7 copy.71
  56.6 19.2 %all-gather.6.cloned.1.call-done = bf16[2048,768]{1,0:T(8,128)(2,1)} async-done(((bf16[512,768]{1,0:T(8,128)(2,1)}), bf16[2048,768]{1,0:T(8,128)(2,1)}) %all-gather.6.cloned.1.call-update) | async-done | bytes 3145744 | tf_op jit(solution)/shard_map/all_gather | solution.py:82
  75.8 4.7 copy.69
  80.5 6.5 copy.72
  88.0 85.2 %while.28 = (s32[]{:T(128)}, bf16[12,512,64]{1,2,0:T(8,128)(2,1)}, f32[12,512]{1,0:T(8,128)}, bf16[12,512,64]{2,1,0:T(8,128)(2,1)S(1)}, bf16[12,2048,64]{2,1,0:T...) while((s32[]{:T(128)}, bf16[12,512,64]{1,2,0:T(8,128)(2,1)}, ...), condition=%wide.region_8.9_spmd.clone, body=%wide.region_5.8_spmd.clone.sunk | while | flops 279969280 | bytes 13928569 | solution.py:101
  179.5 4.6 reshape.380
  184.1 7.8 scatter_custom_fusion
  191.9 51.8 %all_to_all.20 = bf16[8,160,768]{2,1,0:T(8,128)(2,1)} all-to-all(bf16[8,160,768]{2,1,0:T(8,128)(2,1)} %bitcast.190), channel_id=1, replica_groups=mesh['expert'=8,'hidden'=4] {'expert'}, dimensions={0} | all-to-all | bytes 3932160 | tf_op jit(solution)/shard_map/all_to_all | solution.py:126
  243.7 3.6 mul.270
  247.3 5.5 mul.277
  254.9 7.8 scatter_custom_fusion.1
  262.7 49.3 %all_to_all.21 = bf16[8,160,768]{2,1,0:T(8,128)(2,1)} all-to-all(bf16[8,160,768]{2,1,0:T(8,128)(2,1)} %bitcast.189), channel_id=1, replica_groups=mesh['expert'=8,'hidden'=4] {'expert'}, dimensions={0} | all-to-all | bytes 3932160 | tf_op jit(solution)/shard_map/all_to_all | solution.py:164
  313.8 42.8 %collective-permute-done = bf16[1280,768]{1,0:T(8,128)(2,1)} collective-permute-done((bf16[1280,768]{1,0:T(8,128)(2,1)}, bf16[1280,768]{1,0:T(8,128)(2,1)}, u32[]{:S(2)}, u32[]{:S(2)}) %collective-permute-start) | collective-permute-done | bytes 1966112 | tf_op jit(solution)/shard_map/ppermute | solution.py:175
  356.6 3.7 broadcast_in_dim.32
  366.2 3.0 constant_dynamic-update-slice_fusion.1
  369.2 11.8 %collective-permute-done.2 = bf16[1280,768]{1,0:T(8,128)(2,1)} collective-permute-done((bf16[1280,768]{1,0:T(8,128)(2,1)}, bf16[1280,768]{1,0:T(8,128)(2,1)}, u32[]{:S(2)}, u32[]{:S(2)}) %collective-permute-start.2) | collective-permute-done | bytes 1966112 | tf_op jit(solution)/shard_map/ppermute | solution.py:175
  384.0 12.8 %fusion.72 = f32[5120,768]{1,0:T(8,128)} fusion(bf16[5120,768]{1,0:T(8,128)(2,1)} %all-gather.8.cloned.1.call-done, bf16[1,768,768]{2,1,0:T(8,128)(2,1)S(1)} %copy-done), kind=kOutput, calls=%fused_computation.115 | convolution fusion | flops 6039797760 | bytes 24772608 | tf_op jit(solution)/shard_map/dot_general | solution.py:16
  396.7 19.0 %fusion.50 = bf16[5120,768]{1,0:T(8,128)(2,1)S(1)} fusion(f32[5120,768]{1,0:T(8,128)} %fusion.72, bf16[5120,768]{1,0:T(8,128)(2,1)} %constant_dynamic-update-slice_fusion, bf16[1,768,768]{2,1,0:T(8,128)(2,1)S(1)} %copy-done.47), kind=kOutput, calls=%fused_computation.67 | convolution fusion | flops 6118440960 | bytes 32636928 | tf_op jit(solution)/shard_map/dot_general | solution.py:20
  415.7 3.2 copy-done.56
  418.9 8.6 convolution_convert_fusion
  428.8 16.1 %convolution_convert_fusion.1 = bf16[5120,768]{1,0:T(8,128)(2,1)} fusion(bf16[1,768,768]{2,1,0:T(8,128)(2,1)S(1)} %copy-done.48, f32[5120,768]{1,0:T(8,128)} %fusion.72), kind=kOutput, calls=%fused_computation.70 | convolution fusion | flops 6079119360 | bytes 24772608 | tf_op jit(solution)/shard_map/dot_general | solution.py:16
  444.9 49.5 %reduce-scatter.7.cloned.1.call-done = bf16[1280,768]{1,0:T(8,128)(2,1)} async-done(((bf16[5120,768]{1,0:T(8,128)(2,1)}), bf16[1280,768]{1,0:T(8,128)(2,1)}) %reduce-scatter.7.cloned.1.call-update) | async-done | bytes 1966096 | tf_op jit(solution)/shard_map/reduce_scatter | solution.py:190
  494.4 5.5 all-to-all-start.3
  500.0 66.1 %reduce-scatter.5.cloned.1.call-done = bf16[1280,768]{1,0:T(8,128)(2,1)} async-done(((bf16[5120,768]{1,0:T(8,128)(2,1)}), bf16[1280,768]{1,0:T(8,128)(2,1)}) %reduce-scatter.5.cloned.1.call-update) | async-done | bytes 1966096 | tf_op jit(solution)/shard_map/reduce_scatter | solution.py:133
  566.0 5.5 all-to-all-start.1
  574.0 14.3 %gather_fusion.1 = bf16[1024,768]{1,0:T(8,128)(2,1)} fusion(bf16[8,160,768]{2,1,0:T(8,128)(2,1)S(1)} %all-to-all-done.3, s32[1024]{0:T(1024)S(1)} %bitcast.184), kind=kCustom, calls=%fused_computation.1 | custom fusion | bytes 3153920 | tf_op jit(solution)/shard_map/gather | solution.py:203
  588.3 4.9 reshape.365
  593.2 23.9 %all-to-all-done.1 = bf16[8,160,768]{2,1,0:T(8,128)(2,1)} async-done(((bf16[8,160,768]{2,1,0:T(8,128)(2,1)}), bf16[8,160,768]{2,1,0:T(8,128)(2,1)}, u32[]{:S(2)}, u32[]{:S(2)}) %all-to-all-start.1) | async-done | bytes 1966112 | tf_op jit(solution)/shard_map/all_to_all | solution.py:136
  617.1 14.6 %gather_fusion = bf16[1024,768]{1,0:T(8,128)(2,1)S(1)} fusion(bf16[8,160,768]{2,1,0:T(8,128)(2,1)} %all-to-all-done.1, s32[1024]{0:T(1024)S(1)} %bitcast.185), kind=kCustom, calls=%fused_computation | custom fusion | bytes 3153920 | tf_op jit(solution)/shard_map/gather | solution.py:144
  634.4 9.7 multiply_reduce_fusion.1
  645.0 5.6 reduce_sum.241
  655.6 133.3 %while.29 = (s32[]{:T(128)}, bf16[12,512,64]{1,2,0:T(8,128)(2,1)S(1)}, bf16[12,2048,64]{1,2,0:T(8,128)(2,1)}, bf16[12,2048,64]{1,2,0:T(8,128)(2,1)}, bf16[12,512...) while((s32[]{:T(128)}, ...), condition=%wide.region_30.31_spmd.clone, body=%wide.region_28.30_spmd.clone.sunk | while | flops 683834880 | bytes 34630792 | solution.py:229
  658.1 3.0 multiply_reduce_fusion.11
  669.3 3.0 multiply_reduce_fusion.11
  702.6 3.0 multiply_reduce_fusion.11
  736.0 3.0 multiply_reduce_fusion.11
  794.9 30.4 %reduce-scatter.9.cloned.1.call-done = bf16[512,768]{0,1:T(8,128)(2,1)} async-done(((bf16[2048,768]{0,1:T(8,128)(2,1)}), bf16[512,768]{0,1:T(8,128)(2,1)}) %reduce-scatter.9.cloned.1.call-update) | async-done | bytes 786448 | tf_op jit(solution)/shard_map/reduce_scatter | solution.py:240
  825.2 3.6 fusion.87
  828.8 37.1 %reduce-scatter.11.cloned.1.call-done = bf16[512,768]{0,1:T(8,128)(2,1)} async-done(((bf16[2048,768]{0,1:T(8,128)(2,1)}), bf16[512,768]{0,1:T(8,128)(2,1)}) %reduce-scatter.11.cloned.1.call-update) | async-done | bytes 786448 | tf_op jit(solution)/shard_map/reduce_scatter | solution.py:243
  865.9 3.6 fusion.85
  869.6 12.2 %multiply_bitcast_fusion.1 = f32[1,768,768]{2,1,0:T(8,128)} fusion(bf16[5120,768]{1,0:T(8,128)(2,1)} %all-gather.8.cloned.1.call-done, bf16[5120,768]{1,0:T(8,128)(2,1)} %copy-done.56, f32[]{:T(128)S(6)} %convert_element_type.180), kind=kOutput, calls=%fused_computation.78 | convolution fusion | flops 6040387584 | bytes 18087940 | tf_op jit(solution)/shard_map/dot_general | solution.py:20
  881.8 14.4 %multiply_bitcast_fusion = f32[1,768,768]{2,1,0:T(8,128)} fusion(bf16[5120,768]{1,0:T(8,128)(2,1)} %constant_dynamic-update-slice_fusion, f32[]{:T(128)S(6)} %convert_element_type.180, f32[5120,768]{1,0:T(8,128)} %fusion.72), kind=kOutput, calls=%fused_computation.77 | convolution fusion | flops 6075777024 | bytes 25952260 | tf_op jit(solution)/shard_map/dot_general | solution.py:20
  902.2 41.3 %all-reduce = (f32[768]{0:T(1024)}, f32[768]{0:T(1024)}, f32[768]{0:T(1024)}, f32[768]{0:T(1024)}, f32[768,8]{0,1:T(8,128)}, /*index=5*/f32[8]{0:T(128)S(1)}) all-reduce(f32[768]{0:T(1024)S(1)} %get-tuple-element.230, f32[768]{0:T(1024)S(1)} %get-tuple-element.235, ...), channel_id=1, replica_groups=mesh['expert'=8,'hidden'=4] {'expert','hidden'}, use_global_device_ids=true, to_apply=%region_36.37 | all-reduce | flops 9224 | bytes 73792 | tf_op jit(solution)/shard_map/psum | solution.py:263
  946.9 119.1 %all-reduce.4.cloned.1.call-done = (f32[768,768]{1,0:T(8,128)}, f32[768,768]{1,0:T(8,128)}, f32[768,768]{1,0:T(8,128)}, f32[768,768]{1,0:T(8,128)}) async-done(((f32[768,768]{1,0:T(8,128)}, f32[768,768]{1,0:T(8,128)}, f32[768,768]{1,0:T(8,128)}, f32[768,768]{1,0:T(8,128)}), (f32[768,768]{1,0:T(8,128)}, f32[768,768]{1,0:T(8,128)}, f32[768,768]{1,0:T(8,128)}, ...) | async-done | bytes 9437200 | tf_op jit(solution)/shard_map/psum | solution.py:263
  1066.0 3.4 copy.125
  (346 shorter events, 280.4 us)
Async XLA Ops:
  7.2 376.8 %copy-start = (bf16[1,768,768]{2,1,0:T(8,128)(2,1)S(1)}, bf16[1,768,768]{2,1,0:T(8,128)(2,1)}, u32[]{:S(2)}) copy-start(bf16[1,768,768]{2,1,0:T(8,128)(2,1)} %param.31) | copy-start | bytes 3538948
  7.2 37.9 %all-gather.4.cloned.1.call-start = ((), (), s32[]{:S(2)}) async-start(), calls=%async_computation.8 | async-start | bytes 3932160 | tf_op jit(solution)/shard_map/all_gather | solution.py:81
  8.6 11.8 %copy-start.27 = (f32[512]{0:T(512)}, f32[512]{0:T(512)S(1)}, u32[]{:S(2)}) copy-start(f32[512]{0:T(512)S(1)} %broadcast_multiply_fusion.5) | copy-start | bytes 6148
  10.2 10.3 copy-start.33
  10.2 3.6 copy-start.3
  10.2 3.6 copy-start.16
  10.2 3.6 copy-start.37
  10.2 3.6 copy-start.53
  13.7 3.0 copy-start.55
  13.7 62.1 %all-gather.6.cloned.1.call-start = ((), (), s32[]{:S(2)}) async-start(), calls=%async_computation.9 | async-start | bytes 3932160 | tf_op jit(solution)/shard_map/all_gather | solution.py:82
  15.6 368.3 %all-gather.8.cloned.1.call-start = ((), (), s32[]{:S(2)}) async-start(), calls=%async_computation.10 | async-start | bytes 9830400 | tf_op jit(solution)/shard_map/all_gather | solution.py:129
  25.6 5.1 copy-start.39
  80.5 7.5 copy-start.40
  173.2 3.6 copy-start.44
  174.4 2.8 copy-start.23
  174.4 2.8 copy-start.43
  177.5 75.3 %copy-start.5 = (bf16[512,768]{1,0:T(8,128)(2,1)}, bf16[512,768]{1,0:T(8,128)(2,1)S(1)}, u32[]{:S(2)}) copy-start(bf16[512,768]{1,0:T(8,128)(2,1)S(1)} %add_convert_fusion.1) | copy-start | bytes 2359300
  243.7 250.8 %reduce-scatter.7.cloned.1.call-start = ((), (), s32[]{:S(2)}) async-start(), calls=%async_computation.12 | async-start | bytes 9830400 | tf_op jit(solution)/shard_map/reduce_scatter | solution.py:190
  254.7 8.0 copy-start.14
  312.1 44.6 %collective-permute-start = (bf16[1280,768]{1,0:T(8,128)(2,1)}, bf16[1280,768]{1,0:T(8,128)(2,1)}, u32[]{:S(2)}, u32[]{:S(2)}) collective-permute-start(bf16[1280,768]{1,0:T(8,128)(2,1)} %bitcast.19), channel_id=1, source_target_pairs={{0,1},{1,2},{2,3},{3,0},{4,5},{5,6},{6,7},{7,4},{8,9},{9,10},{10,1... | collective-permute-start | bytes 5898248 | tf_op jit(solution)/shard_map/ppermute | solution.py:175
  312.1 54.2 %collective-permute-start.1 = (bf16[1280,768]{1,0:T(8,128)(2,1)}, bf16[1280,768]{1,0:T(8,128)(2,1)}, u32[]{:S(2)}, u32[]{:S(2)}) collective-permute-start(bf16[1280,768]{1,0:T(8,128)(2,1)} %bitcast.19), channel_id=1, source_target_pairs={{0,3},{1,0},{2,1},{3,2},{4,7},{5,4},{6,5},{7,6},{8,11},{9,8},{10,9... | collective-permute-start | bytes 5898248 | tf_op jit(solution)/shard_map/ppermute | solution.py:178
  356.6 24.4 %collective-permute-start.2 = (bf16[1280,768]{1,0:T(8,128)(2,1)}, bf16[1280,768]{1,0:T(8,128)(2,1)}, u32[]{:S(2)}, u32[]{:S(2)}) collective-permute-start(bf16[1280,768]{1,0:T(8,128)(2,1)} %collective-permute-done), channel_id=1, source_target_pairs={{0,1},{1,2},{2,3},{3,0},{4,5},{5,6},{6,7},{7,4},{8,9},{9,10},{10,1... | collective-permute-start | bytes 5898248 | tf_op jit(solution)/shard_map/ppermute | solution.py:175
  384.0 12.8 %copy-start.47 = (bf16[1,768,768]{2,1,0:T(8,128)(2,1)S(1)}, bf16[1,768,768]{2,1,0:T(8,128)(2,1)}, u32[]{:S(2)}) copy-start(bf16[1,768,768]{2,1,0:T(8,128)(2,1)} %param.32) | copy-start | bytes 3538948
  415.7 3.2 copy-start.56
  427.6 138.5 %reduce-scatter.5.cloned.1.call-start = ((), (), s32[]{:S(2)}) async-start(), calls=%async_computation.11 | async-start | bytes 9830400 | tf_op jit(solution)/shard_map/reduce_scatter | solution.py:133
  494.4 71.6 %all-to-all-start.3 = ((bf16[8,160,768]{2,1,0:T(8,128)(2,1)}), bf16[8,160,768]{2,1,0:T(8,128)(2,1)S(1)}, u32[]{:S(2)}, u32[]{:S(2)}) async-start(bf16[8,160,768]{2,1,0:T(8,128)(2,1)} %bitcast.198), calls=%async_computation.5 | async-start | bytes 3932160 | tf_op jit(solution)/shard_map/all_to_all | solution.py:195
  566.0 51.0 %all-to-all-start.1 = ((bf16[8,160,768]{2,1,0:T(8,128)(2,1)}), bf16[8,160,768]{2,1,0:T(8,128)(2,1)}, u32[]{:S(2)}, u32[]{:S(2)}) async-start(bf16[8,160,768]{2,1,0:T(8,128)(2,1)} %bitcast.197), calls=%async_computation.2 | async-start | bytes 3932160 | tf_op jit(solution)/shard_map/all_to_all | solution.py:136
  571.5 253.7 %reduce-scatter.9.cloned.1.call-start = ((), (), s32[]{:S(2)}) async-start(), calls=%async_computation.13 | async-start | bytes 3932160 | tf_op jit(solution)/shard_map/reduce_scatter | solution.py:240
  631.7 2.8 copy-start.15
  634.4 9.8 copy-start.30
  634.4 9.9 copy-start.26
  645.0 5.6 copy-start.20
  645.0 5.6 copy-start.22
  645.0 5.7 copy-start.24
  645.0 5.7 copy-start.32
  789.1 76.9 %reduce-scatter.11.cloned.1.call-start = ((), (), s32[]{:S(2)}) async-start(), calls=%async_computation.14 | async-start | bytes 3932160 | tf_op jit(solution)/shard_map/reduce_scatter | solution.py:243
  789.8 276.1 %all-reduce.4.cloned.1.call-start = ((), (), s32[]{:S(2)}) async-start(), calls=%async_computation.15 | async-start | bytes 18874368 | tf_op jit(solution)/shard_map/psum | solution.py:263
  790.2 2.5 copy-start.10
  881.8 14.4 %copy-start.6 = (bf16[512,768]{1,0:T(8,128)(2,1)S(1)}, bf16[512,768]{1,0:T(8,128)(2,1)}, u32[]{:S(2)}) copy-start(bf16[512,768]{1,0:T(8,128)(2,1)} %copy-done.5) | copy-start | bytes 2359300
  881.8 14.4 %copy-start.21 = (f32[512,8]{0,1:T(8,128)S(1)}, f32[512,8]{0,1:T(8,128)}, u32[]{:S(2)}) copy-start(f32[512,8]{0,1:T(8,128)} %copy-done.20) | copy-start | bytes 49156
  881.8 14.8 %copy-start.50 = (bf16[768,768]{1,0:T(8,128)(2,1)S(1)}, bf16[768,768]{1,0:T(8,128)(2,1)}, u32[]{:S(2)}) copy-start(bf16[768,768]{1,0:T(8,128)(2,1)} %param.24) | copy-start | bytes 3538948
  899.6 2.6 copy-start.35
  899.6 2.6 copy-start.36
  899.6 2.6 copy-start.46
  1066.0 3.4 copy-start.13
  1069.3 2.5 copy-start.12
  1071.9 2.5 copy-start.11
  1071.9 3.9 copy-start.1
  (22 other events, 29.4 us)
Sparse Core Ops, SparseCore 0:
  13.8 31.2 all-gather.3
  47.2 28.5 all-gather.5
  243.8 53.0 all-gather.7
  427.7 66.6 reduce-scatter.6
  497.0 69.0 reduce-scatter.4
  789.1 36.0 reduce-scatter.8
  827.9 37.9 reduce-scatter.10
  872.8 193.1 all-reduce.3
